TPU v7x, 32 devices: a whole 2x2x4 slice. The times are simulated.
32 devices in a mesh: prow: 8 (over y, x, core), pcol: 4 (over z).
Axes of the slice: x: 2, y: 2, z: 4, core: 2. Of those that a mesh axis runs over, the one named last changes fastest.
Arguments:
- cov_trail: float32 [1024, 1024], P('prow', 'pcol'), as said below
- factor_panel: bfloat16 [4, 1024, 128], P(None, 'prow'), may hold values from -0.25 to 0.25
- first_level: int32 [8], replicated, may hold values from 0 to 4
- block_slot: int32 [8], replicated, may hold values from 0 to 7, each once
- factor_window: bfloat16 [6, 128, 128], replicated, may hold values from -0.5 to 0.5
- diag_inverse: float32 [4, 128, 128], replicated, as said below
Outputs:
- panel_cov: float32 [4, 1024, 128], P(None, 'prow')
- window_cov: float32 [512, 512], replicated
Inputs may be any that keep to these rules, and one draw needn't show every extreme that they name: Trailing block j lies in the pattern of window supernode k exactly when first_level[j] <= k, so the patterns are nested. `block_slot`: a permutation; slot s is held by process row s // 1 and process column s // (8 / pcol size), slots in contiguous blocks. `cov_trail`: symmetric. `diag_inverse`: each block symmetric.
All inputs are finite; a program needn't handle non-finite values.
Results may differ from a plain program's by a relative error of at most 0.0003.
Values may be sent and summed in bfloat16 or wider, within the bound.
A program may use at most 64 MiB of HBM per device.

v0:
```python
import jax
import jax.numpy as jnp
from jax import lax
from jax.sharding import PartitionSpec as P


def pair_index(upper, lower, window_count):
    return lower * window_count - lower * (lower + 1) // 2 + upper - lower - 1


def later_block(window, upper, lower):
    if upper >= lower:
        return window[upper, lower]
    return window[lower, upper].T


def window_step(window, cross_sums, diag_term, later_nodes, window_factor, diag_block, supernode):
    highest = lax.Precision.HIGHEST
    for place, upper in enumerate(later_nodes):
        block_total = cross_sums[place]
        for second, other in enumerate(later_nodes):
            block_total = block_total + jnp.dot(
                later_block(window, upper, other),
                window_factor[second],
                precision=highest,
                preferred_element_type=jnp.float32,
            )
        window[upper, supernode] = -block_total
    diagonal = diag_block - diag_term
    for place, upper in enumerate(later_nodes):
        diagonal = diagonal - jnp.dot(
            window_factor[place].T,
            window[upper, supernode],
            precision=highest,
            preferred_element_type=jnp.float32,
        )
    window[supernode, supernode] = diagonal


def shards(cov_trail, factor_panel, first_level, block_slot, factor_window, diag_inverse):
    highest = lax.Precision.HIGHEST
    block_size = diag_inverse.shape[-1]
    window_count = diag_inverse.shape[0]
    rows_loc = cov_trail.shape[0]
    cols_loc = cov_trail.shape[1]
    block_count = first_level.shape[0]
    slot_ids = lax.iota(jnp.int32, block_count)
    level_slot = jnp.sum(
        jnp.where(block_slot[None, :] == slot_ids[:, None], first_level[None, :], 0), axis=1
    )
    local_blocks = rows_loc // block_size
    row_level = jnp.repeat(
        lax.dynamic_slice_in_dim(level_slot, lax.axis_index("prow") * local_blocks, local_blocks),
        block_size,
    )
    columns = {}
    window = {}
    for supernode in range(window_count - 1, -1, -1):
        keep_rows = (row_level <= supernode)[:, None]
        panel_row = jnp.where(keep_rows, factor_panel[supernode], jnp.zeros((), jnp.bfloat16))
        gathered = lax.all_gather(panel_row, "prow", axis=0, tiled=True)
        panel_col = lax.dynamic_slice_in_dim(
            gathered, lax.axis_index("pcol") * cols_loc, cols_loc, 0
        )
        panel_full = panel_row.astype(jnp.float32)
        partial_prod = jnp.dot(
            cov_trail,
            panel_col.astype(jnp.float32),
            precision=highest,
            preferred_element_type=jnp.float32,
        )
        later_nodes = list(range(supernode + 1, window_count))
        window_factor = [
            factor_window[pair_index(upper, supernode, window_count)].astype(jnp.float32)
            for upper in later_nodes
        ]
        summed = lax.psum(partial_prod, "pcol")
        accumulated = summed
        for place, upper in enumerate(later_nodes):
            accumulated = accumulated + jnp.dot(
                columns[upper],
                window_factor[place],
                precision=highest,
                preferred_element_type=jnp.float32,
            )
        new_column = jnp.where(keep_rows, -accumulated, jnp.float32(0.0))
        columns[supernode] = new_column
        term_list = []
        for upper in later_nodes:
            term_list.append(
                jnp.dot(
                    columns[upper].T,
                    panel_full,
                    precision=highest,
                    preferred_element_type=jnp.float32,
                )
            )
        term_list.append(
            jnp.dot(panel_full.T, new_column, precision=highest, preferred_element_type=jnp.float32)
        )
        cross_sums = lax.psum(jnp.stack(term_list), "prow")
        diag_term = cross_sums[len(later_nodes)]
        window_step(
            window,
            cross_sums,
            diag_term,
            later_nodes,
            window_factor,
            diag_inverse[supernode],
            supernode,
        )
    panel_cov = jnp.stack([columns[supernode] for supernode in range(window_count)])
    block_rows = [
        jnp.concatenate(
            [later_block(window, upper, other) for other in range(window_count)], axis=1
        )
        for upper in range(window_count)
    ]
    window_cov = jnp.concatenate(block_rows, axis=0)
    return (panel_cov, window_cov)


def solution(mesh):
    return jax.shard_map(
        shards,
        mesh=mesh,
        in_specs=(P("prow", "pcol"), P(None, "prow", None), P(), P(), P(), P()),
        out_specs=(P(None, "prow", None), P()),
        check_vma=False,
    )
```

profile of v0, /device:TPU:0, one launch (start us, length us, event | category | flops | bytes accessed | tf_op | source)
XLA Modules:
  0.0 169.3 jit_solution(11450177156620109265)
XLA Ops:
  7.3 0.7 copy-done.9
  8.0 0.6 dynamic_slice.15
  11.2 0.8 slice_select_fusion.3
  12.1 10.8 %all-gather.3 = bf16[1,1024,128]{2,1,0:T(8,128)(2,1)S(1)} all-gather(bf16[1,128,128]{2,1,0:T(8,128)(2,1)S(1)} %get-tuple-element.20), channel_id=5, replica_groups=mesh['prow'=8,'pcol'=4] {'prow'}, dimensions={1}, use_global_device_ids=true | all-gather | bytes 294912 | tf_op jit(solution)/shard_map/all_gather | solution.py:61
  22.8 9.3 %all-gather.2 = bf16[1,1024,128]{2,1,0:T(8,128)(2,1)S(1)} all-gather(bf16[1,128,128]{2,1,0:T(8,128)(2,1)S(1)} %get-tuple-element.21), channel_id=4, replica_groups=mesh['prow'=8,'pcol'=4] {'prow'}, dimensions={1}, use_global_device_ids=true | all-gather | bytes 294912 | tf_op jit(solution)/shard_map/all_gather | solution.py:61
  32.1 0.9 convolution_bitcast_fusion.16
  33.0 0.9 convolution_bitcast_fusion.17
  33.9 8.3 %all-gather.1 = bf16[1,1024,128]{2,1,0:T(8,128)(2,1)S(1)} all-gather(bf16[1,128,128]{2,1,0:T(8,128)(2,1)S(1)} %get-tuple-element.19), channel_id=3, replica_groups=mesh['prow'=8,'pcol'=4] {'prow'}, dimensions={1}, use_global_device_ids=true | all-gather | bytes 294912 | tf_op jit(solution)/shard_map/all_gather | solution.py:61
  42.2 0.9 convolution_bitcast_fusion.18
  43.1 9.3 %all-gather = bf16[1,1024,128]{2,1,0:T(8,128)(2,1)S(1)} all-gather(bf16[1,128,128]{2,1,0:T(8,128)(2,1)S(1)} %get-tuple-element.18), channel_id=2, replica_groups=mesh['prow'=8,'pcol'=4] {'prow'}, dimensions={1}, use_global_device_ids=true | all-gather | bytes 294912 | tf_op jit(solution)/shard_map/all_gather | solution.py:61
  52.4 0.9 convolution_bitcast_fusion.19
  53.3 36.4 %all-reduce.7.cloned.1.call-done = (f32[128,128]{0,1:T(8,128)}, f32[128,128]{0,1:T(8,128)}, f32[128,128]{0,1:T(8,128)}, f32[128,128]{0,1:T(8,128)}) async-done(((f32[128,128]{0,1:T(8,128)}, f32[128,128]{0,1:T(8,128)}, f32[128,128]{0,1:T(8,128)}, f32[128,128]{0,1:T(8,128)}), (f32[128,128]{0,1:T(8,128)}, f32[128,128]{0,1:T(8,128)}, f32[128,128]{0,1:T(8,128)}, ...) | async-done | bytes 262160 | tf_op jit(solution)/shard_map/psum | solution.py:77
  89.7 1.1 fusion.17
  91.2 0.6 copy-done.1
  93.6 1.7 convolution_bitcast_fusion.6
  95.7 0.2 fusion.13
  96.2 0.7 pad_maximum_fusion.4
  96.9 0.7 pad_maximum_fusion.3
  97.5 0.7 pad_maximum_fusion.1
  98.3 0.8 copy.67
  99.2 54.7 %all-reduce.5.cloned.1.call-done = (f32[1,128,128]{2,1,0:T(8,128)}, f32[2,128,128]{1,2,0:T(8,128)}, f32[3,128,128]{2,1,0:T(8,128)}, f32[4,128,128]{2,1,0:T(8,128)}) async-done(((f32[1,128,128]{2,1,0:T(8,128)}, f32[2,128,128]{1,2,0:T(8,128)}, f32[3,128,128]{2,1,0:T(8,128)}, f32[4,128,128]{2,1,0:T(8,128)}), (f32[1,128,128]{2,1,0:T(8,128)}, f32[2,128,128]{1,2,0:T(8,128)}, f32[3,128,128]{2,1,0:T(8,128)}, ...) | async-done | bytes 655376 | tf_op jit(solution)/shard_map/psum | solution.py:101
  153.8 1.0 fusion.103
  155.2 0.6 copy-done.5
  155.7 0.2 convolution_add_fusion.10
  156.4 0.2 convolution_add_fusion.12
  156.9 0.4 copy-done.3
  157.5 0.2 convolution_add_fusion.1
  158.9 0.2 convolution_add_fusion.8
  159.4 0.2 fusion.5
  160.4 0.2 fusion.3
  160.7 0.2 fusion.2
  161.4 1.1 maximum_maximum_fusion
  (61 shorter events, 6.7 us)
Async XLA Ops:
  7.2 24.9 %copy-start = (f32[128,256]{1,0:T(8,128)S(1)}, f32[128,256]{1,0:T(8,128)}, u32[]{:S(2)}) copy-start(f32[128,256]{1,0:T(8,128)} %param.6) | copy-start | bytes 393220
  7.2 82.6 %all-reduce.7.cloned.1.call-start = ((), (), s32[]{:S(2)}) async-start(), calls=%async_computation.1 | async-start | bytes 524288 | tf_op jit(solution)/shard_map/psum | solution.py:77
  7.2 0.7 copy-start.9
  7.2 0.7 copy-start.10
  53.3 36.5 %copy-start.2 = (bf16[6,128,128]{2,1,0:T(8,128)(2,1)S(1)}, bf16[6,128,128]{2,1,0:T(8,128)(2,1)}, u32[]{:S(2)}) copy-start(bf16[6,128,128]{2,1,0:T(8,128)(2,1)} %param.10) | copy-start | bytes 589828
  53.3 100.6 %all-reduce.5.cloned.1.call-start = ((), (), s32[]{:S(2)}) async-start(), calls=%async_computation | async-start | bytes 1310720 | tf_op jit(solution)/shard_map/psum | solution.py:101
  89.7 1.2 copy-start.8
  90.9 0.8 copy-start.1
  93.6 1.7 copy-start.7
  98.3 55.5 %copy-start.4 = (f32[4,128,128]{2,1,0:T(8,128)S(1)}, f32[4,128,128]{2,1,0:T(8,128)}, u32[]{:S(2)}) copy-start(f32[4,128,128]{2,1,0:T(8,128)} %param.11) | copy-start | bytes 786436
  153.8 1.0 copy-start.6
  154.8 0.9 copy-start.5
  156.4 1.0 copy-start.3
Sparse Core Ops, SparseCore 0:
  53.4 36.2 all-reduce.6
  98.4 55.3 all-reduce.4
where the time goes:
time: 170 us; the launch traced here: 169 us
  waiting for transfers between devices  91.1 us (54%)
  blocking collectives  37.6 us (22%)
  between operations  17.1 us (10%)
  matrix products  13.7 us (8%)
  other arithmetic  5.08 us (3%)
  local copies, waits for them, and re-layouts  4.56 us (3%)
    psum x1, waiting for transfers between devices, shards(): cross_sums = lax.psum(jnp.stack(term_list), 'prow')  54.7 us
    all_gather x4, blocking collectives, shards(): gathered = lax.all_gather(panel_row, 'prow', axis=0, tiled=True)  37.6 us
    psum x1, waiting for transfers between devices, shards(): summed = lax.psum(partial_prod, 'pcol')  36.4 us
    dot_general x4, matrix products, shards(): jnp.dot(cov_trail, panel_col.astype(jnp.float32), precision=highest, pref...  3.55 us
    unnamed x26, local copies, waits for them, and re-layouts  3.41 us
  transfers between devices with their start and end apart: 2, of which 2 were waited for; matrix products, arithmetic and copies ran while one was open for 1% of the time, Pallas kernels for 0%

commit v1 on v0

--- a/solution.py
+++ b/solution.py
@@ -2,6 +2,24 @@
 import jax.numpy as jnp
 from jax import lax
 from jax.sharding import PartitionSpec as P
+
+
+def laid_out(tiles, dim):
+    tiles = jnp.moveaxis(tiles, 0, dim)
+    dims = tiles.shape
+    return tiles.reshape(*dims[:dim], dims[dim] * dims[dim + 1], *dims[dim + 2 :])
+
+
+def doubled(value, axis):
+    size = lax.axis_size(axis)
+    blocks = value[None]
+    for level in range(size.bit_length() - 1):
+        bit = 1 << level
+        other = lax.ppermute(blocks, axis, [(i, i ^ bit) for i in range(size)])
+        both = jnp.stack([blocks, other])
+        upper = lax.axis_index(axis) >> level & 1
+        blocks = jnp.where(upper == 0, both, both[::-1]).reshape(-1, *value.shape)
+    return blocks
 
 
 def pair_index(upper, lower, window_count):
@@ -58,7 +76,7 @@
     for supernode in range(window_count - 1, -1, -1):
         keep_rows = (row_level <= supernode)[:, None]
         panel_row = jnp.where(keep_rows, factor_panel[supernode], jnp.zeros((), jnp.bfloat16))
-        gathered = lax.all_gather(panel_row, "prow", axis=0, tiled=True)
+        gathered = laid_out(doubled(panel_row, "prow"), 0)
         panel_col = lax.dynamic_slice_in_dim(
             gathered, lax.axis_index("pcol") * cols_loc, cols_loc, 0
         )

time: 170 us -> 156 us (0.918)
  blocking collectives: 37.6 us -> 0 us
  waiting for transfers between devices: 91.1 us -> 104 us
  starting transfers between devices: 0.08 us -> 10.3 us
    all_gather x4 -> x0, blocking collectives: 37.6 us -> none  [shards(): gathered = lax.all_gather(panel_row, 'prow', axis=0, tiled=True)]
    ppermute x0 -> x12, waiting for transfers between devices: none -> 11.7 us  [doubled(): other = lax.ppermute(blocks, axis, [(i, i ^ bit) for i in range(size)])]
    ppermute x0 -> x12, starting transfers between devices: none -> 10.2 us  [doubled(): other = lax.ppermute(blocks, axis, [(i, i ^ bit) for i in range(size)])]
    unnamed x26 -> x28, local copies, waits for them, and re-layouts: 3.41 us -> 4.06 us
  transfers between devices with their start and end apart: 2 -> 14, of which waited for: 2 -> 11; matrix products, arithmetic and copies ran while one was open for 1% -> 3% of each run, Pallas kernels for 0% -> 0%
where the time goes in v1:
time: 156 us
  waiting for transfers between devices  104 us (67%)
  between operations  17.2 us (11%)
  matrix products  13 us (8%)
  starting transfers between devices  10.3 us (7%)
  other arithmetic  5.69 us (4%)
  local copies, waits for them, and re-layouts  5.21 us (3%)
    psum x1, waiting for transfers between devices, shards(): cross_sums = lax.psum(jnp.stack(term_list), 'prow')  54.7 us
    psum x1, waiting for transfers between devices, shards(): summed = lax.psum(partial_prod, 'pcol')  37.8 us
    ppermute x12, waiting for transfers between devices, doubled(): other = lax.ppermute(blocks, axis, [(i, i ^ bit) for i in range(size)])  11.7 us
    ppermute x12, starting transfers between devices, doubled(): other = lax.ppermute(blocks, axis, [(i, i ^ bit) for i in range(size)])  10.2 us
    unnamed x28, local copies, waits for them, and re-layouts  4.06 us
    dot_general x4, matrix products, shards(): jnp.dot(cov_trail, panel_col.astype(jnp.float32), precision=highest, pref...  3.56 us
  transfers between devices with their start and end apart: 14, of which 11 were waited for; matrix products, arithmetic and copies ran while one was open for 3% of the time, Pallas kernels for 0%

profile of v1, /device:TPU:0, one launch (start us, length us, event | category | flops | bytes accessed | tf_op | source)
XLA Modules:
  0.0 155.5 jit_solution(12669768431566766794)
XLA Ops:
  7.3 0.7 copy-done.10
  8.0 0.6 dynamic_slice.15
  11.2 0.8 slice_select_fusion.3
  12.1 0.5 collective-permute-start.3
  13.4 0.9 collective-permute-done
  14.4 2.7 %collective-permute-start.7 = (bf16[2,128,128]{2,1,0:T(8,128)(2,1)S(1)}, bf16[2,128,128]{2,1,0:T(8,128)(2,1)S(1)}, u32[]{:S(2)}, u32[]{:S(2)}) collective-permute-start(bf16[2,128,128]{2,1,0:T(8,128)(2,1)S(1)} %get-tuple-element.27), channel_id=1, source_target_pairs={{0,8},{4,12},{8,0},{12,4},{16,24},{20,28},{24,16},{28,20},{1,9},{5... | collective-permute-start | bytes 196616 | tf_op jit(solution)/shard_map/ppermute | solution.py:18
  17.3 2.0 %collective-permute-start.4 = (bf16[2,128,128]{2,1,0:T(8,128)(2,1)S(1)}, bf16[2,128,128]{2,1,0:T(8,128)(2,1)S(1)}, u32[]{:S(2)}, u32[]{:S(2)}) collective-permute-start(bf16[2,128,128]{2,1,0:T(8,128)(2,1)S(1)} %get-tuple-element.25), channel_id=1, source_target_pairs={{0,8},{4,12},{8,0},{12,4},{16,24},{20,28},{24,16},{28,20},{1,9},{5... | collective-permute-start | bytes 196616 | tf_op jit(solution)/shard_map/ppermute | solution.py:18
  19.8 3.6 %collective-permute-done.4 = bf16[2,128,128]{2,1,0:T(8,128)(2,1)S(1)} collective-permute-done((bf16[2,128,128]{2,1,0:T(8,128)(2,1)S(1)}, bf16[2,128,128]{2,1,0:T(8,128)(2,1)S(1)}, u32[]{:S(2)}, u32[]{:S(2)}) %collective-permute-start.4) | collective-permute-done | bytes 65568 | tf_op jit(solution)/shard_map/ppermute | solution.py:18
  23.5 0.6 collective-permute-done.1
  24.2 1.7 %collective-permute-start.2 = (bf16[4,128,128]{2,1,0:T(8,128)(2,1)S(1)}, bf16[4,128,128]{2,1,0:T(8,128)(2,1)S(1)}, u32[]{:S(2)}, u32[]{:S(2)}) collective-permute-start(bf16[4,128,128]{2,1,0:T(8,128)(2,1)S(1)} %bitcast.284), channel_id=1, source_target_pairs={{0,16},{4,20},{8,24},{12,28},{16,0},{20,4},{24,8},{28,12},{1,17},{... | collective-permute-start | bytes 393224 | tf_op jit(solution)/shard_map/ppermute | solution.py:18
  25.8 0.4 collective-permute-start.5
  26.3 1.6 %collective-permute-start.8 = (bf16[4,128,128]{2,1,0:T(8,128)(2,1)S(1)}, bf16[4,128,128]{2,1,0:T(8,128)(2,1)S(1)}, u32[]{:S(2)}, u32[]{:S(2)}) collective-permute-start(bf16[4,128,128]{2,1,0:T(8,128)(2,1)S(1)} %bitcast.278), channel_id=1, source_target_pairs={{0,16},{4,20},{8,24},{12,28},{16,0},{20,4},{24,8},{28,12},{1,17},{... | collective-permute-start | bytes 393224 | tf_op jit(solution)/shard_map/ppermute | solution.py:18
  27.9 0.5 collective-permute-start.11
  28.4 2.2 %collective-permute-done.2 = bf16[4,128,128]{2,1,0:T(8,128)(2,1)S(1)} collective-permute-done((bf16[4,128,128]{2,1,0:T(8,128)(2,1)S(1)}, bf16[4,128,128]{2,1,0:T(8,128)(2,1)S(1)}, u32[]{:S(2)}, u32[]{:S(2)}) %collective-permute-start.2) | collective-permute-done | bytes 131104 | tf_op jit(solution)/shard_map/ppermute | solution.py:18
  30.7 2.7 %collective-permute-done.5 = bf16[4,128,128]{2,1,0:T(8,128)(2,1)S(1)} collective-permute-done((bf16[4,128,128]{2,1,0:T(8,128)(2,1)S(1)}, bf16[4,128,128]{2,1,0:T(8,128)(2,1)S(1)}, u32[]{:S(2)}, u32[]{:S(2)}) %collective-permute-start.5) | collective-permute-done | bytes 131104 | tf_op jit(solution)/shard_map/ppermute | solution.py:18
  33.5 0.9 convolution_bitcast_fusion.19
  34.4 0.9 convolution_bitcast_fusion.18
  35.3 0.6 collective-permute-done.8
  36.0 0.9 convolution_bitcast_fusion.17
  37.4 0.9 convolution_bitcast_fusion.16
  38.4 37.8 %all-reduce.7.cloned.1.call-done = (f32[128,128]{0,1:T(8,128)}, f32[128,128]{0,1:T(8,128)}, f32[128,128]{0,1:T(8,128)}, f32[128,128]{0,1:T(8,128)}) async-done(((f32[128,128]{0,1:T(8,128)}, f32[128,128]{0,1:T(8,128)}, f32[128,128]{0,1:T(8,128)}, f32[128,128]{0,1:T(8,128)}), (f32[128,128]{0,1:T(8,128)}, f32[128,128]{0,1:T(8,128)}, f32[128,128]{0,1:T(8,128)}, ...) | async-done | bytes 262160 | tf_op jit(solution)/shard_map/psum | solution.py:95
  76.1 1.8 %convolution_bitcast_fusion.6 = f32[1,128,128]{2,1,0:T(8,128)} fusion(bf16[1,128,128]{2,1,0:T(8,128)(2,1)S(1)} %get-tuple-element.20, f32[128,128]{0,1:T(8,128)} %get-tuple-element.10, pred[]{:T(512)} %bitcast.33), kind=kOutput, calls=%fused_computation.32 | convolution fusion | flops 25198592 | bytes 163841 | tf_op jit(solution)/shard_map/dot_general | solution.py:117
  78.2 0.6 copy-done.8
  80.8 0.6 copy-done.7
  82.5 0.7 pad_maximum_fusion.12
  83.1 0.7 pad_maximum_fusion.7
  83.8 0.7 pad_maximum_fusion.5
  84.6 0.8 copy.71
  85.4 54.7 %all-reduce.5.cloned.1.call-done = (f32[1,128,128]{2,1,0:T(8,128)}, f32[2,128,128]{1,2,0:T(8,128)}, f32[3,128,128]{2,1,0:T(8,128)}, f32[4,128,128]{2,1,0:T(8,128)}) async-done(((f32[1,128,128]{2,1,0:T(8,128)}, f32[2,128,128]{1,2,0:T(8,128)}, f32[3,128,128]{2,1,0:T(8,128)}, f32[4,128,128]{2,1,0:T(8,128)}), (f32[1,128,128]{2,1,0:T(8,128)}, f32[2,128,128]{1,2,0:T(8,128)}, f32[3,128,128]{2,1,0:T(8,128)}, ...) | async-done | bytes 655376 | tf_op jit(solution)/shard_map/psum | solution.py:119
  140.1 1.0 fusion.107
  141.4 0.6 copy-done.5
  147.6 1.1 maximum_maximum_fusion
  (107 shorter events, 11.7 us)
Async XLA Ops:
  7.2 26.4 %copy-start = (f32[128,256]{1,0:T(8,128)S(1)}, f32[128,256]{1,0:T(8,128)}, u32[]{:S(2)}) copy-start(f32[128,256]{1,0:T(8,128)} %param.6) | copy-start | bytes 393220
  7.2 69.0 %all-reduce.7.cloned.1.call-start = ((), (), s32[]{:S(2)}) async-start(), calls=%async_computation.1 | async-start | bytes 524288 | tf_op jit(solution)/shard_map/psum | solution.py:95
  7.2 0.7 copy-start.10
  7.2 0.7 copy-start.11
  12.1 1.4 collective-permute-start.3
  12.6 4.6 %collective-permute-start.9 = (bf16[1,128,128]{2,1,0:T(8,128)(2,1)S(1)}, bf16[1,128,128]{2,1,0:T(8,128)(2,1)S(1)}, u32[]{:S(2)}, u32[]{:S(2)}) collective-permute-start(bf16[1,128,128]{2,1,0:T(8,128)(2,1)S(1)} %get-tuple-element.20), channel_id=1, source_target_pairs={{0,4},{4,0},{8,12},{12,8},{16,20},{20,16},{24,28},{28,24},{1,5},{5... | collective-permute-start | bytes 98312 | tf_op jit(solution)/shard_map/ppermute | solution.py:18
  12.7 1.7 %collective-permute-start.6 = (bf16[1,128,128]{2,1,0:T(8,128)(2,1)S(1)}, bf16[1,128,128]{2,1,0:T(8,128)(2,1)S(1)}, u32[]{:S(2)}, u32[]{:S(2)}) collective-permute-start(bf16[1,128,128]{2,1,0:T(8,128)(2,1)S(1)} %get-tuple-element.21), channel_id=1, source_target_pairs={{0,4},{4,0},{8,12},{12,8},{16,20},{20,16},{24,28},{28,24},{1,5},{5... | collective-permute-start | bytes 98312 | tf_op jit(solution)/shard_map/ppermute | solution.py:18
  13.1 1.2 collective-permute-start
  14.4 5.3 %collective-permute-start.7 = (bf16[2,128,128]{2,1,0:T(8,128)(2,1)S(1)}, bf16[2,128,128]{2,1,0:T(8,128)(2,1)S(1)}, u32[]{:S(2)}, u32[]{:S(2)}) collective-permute-start(bf16[2,128,128]{2,1,0:T(8,128)(2,1)S(1)} %get-tuple-element.27), channel_id=1, source_target_pairs={{0,8},{4,12},{8,0},{12,4},{16,24},{20,28},{24,16},{28,20},{1,9},{5... | collective-permute-start | bytes 196616 | tf_op jit(solution)/shard_map/ppermute | solution.py:18
  17.2 10.7 %collective-permute-start.10 = (bf16[2,128,128]{2,1,0:T(8,128)(2,1)S(1)}, bf16[2,128,128]{2,1,0:T(8,128)(2,1)S(1)}, u32[]{:S(2)}, u32[]{:S(2)}) collective-permute-start(bf16[2,128,128]{2,1,0:T(8,128)(2,1)S(1)} %get-tuple-element.29), channel_id=1, source_target_pairs={{0,8},{4,12},{8,0},{12,4},{16,24},{20,28},{24,16},{28,20},{1,9},{5... | collective-permute-start | bytes 196616 | tf_op jit(solution)/shard_map/ppermute | solution.py:18
  17.3 6.2 %collective-permute-start.4 = (bf16[2,128,128]{2,1,0:T(8,128)(2,1)S(1)}, bf16[2,128,128]{2,1,0:T(8,128)(2,1)S(1)}, u32[]{:S(2)}, u32[]{:S(2)}) collective-permute-start(bf16[2,128,128]{2,1,0:T(8,128)(2,1)S(1)} %get-tuple-element.25), channel_id=1, source_target_pairs={{0,8},{4,12},{8,0},{12,4},{16,24},{20,28},{24,16},{28,20},{1,9},{5... | collective-permute-start | bytes 196616 | tf_op jit(solution)/shard_map/ppermute | solution.py:18
  19.3 4.9 %collective-permute-start.1 = (bf16[2,128,128]{2,1,0:T(8,128)(2,1)S(1)}, bf16[2,128,128]{2,1,0:T(8,128)(2,1)S(1)}, u32[]{:S(2)}, u32[]{:S(2)}) collective-permute-start(bf16[2,128,128]{2,1,0:T(8,128)(2,1)S(1)} %get-tuple-element.23), channel_id=1, source_target_pairs={{0,8},{4,12},{8,0},{12,4},{16,24},{20,28},{24,16},{28,20},{1,9},{5... | collective-permute-start | bytes 196616 | tf_op jit(solution)/shard_map/ppermute | solution.py:18
  24.2 6.4 %collective-permute-start.2 = (bf16[4,128,128]{2,1,0:T(8,128)(2,1)S(1)}, bf16[4,128,128]{2,1,0:T(8,128)(2,1)S(1)}, u32[]{:S(2)}, u32[]{:S(2)}) collective-permute-start(bf16[4,128,128]{2,1,0:T(8,128)(2,1)S(1)} %bitcast.284), channel_id=1, source_target_pairs={{0,16},{4,20},{8,24},{12,28},{16,0},{20,4},{24,8},{28,12},{1,17},{... | collective-permute-start | bytes 393224 | tf_op jit(solution)/shard_map/ppermute | solution.py:18
  25.8 7.6 %collective-permute-start.5 = (bf16[4,128,128]{2,1,0:T(8,128)(2,1)S(1)}, bf16[4,128,128]{2,1,0:T(8,128)(2,1)S(1)}, u32[]{:S(2)}, u32[]{:S(2)}) collective-permute-start(bf16[4,128,128]{2,1,0:T(8,128)(2,1)S(1)} %bitcast.280), channel_id=1, source_target_pairs={{0,16},{4,20},{8,24},{12,28},{16,0},{20,4},{24,8},{28,12},{1,17},{... | collective-permute-start | bytes 393224 | tf_op jit(solution)/shard_map/ppermute | solution.py:18
  26.3 9.6 %collective-permute-start.8 = (bf16[4,128,128]{2,1,0:T(8,128)(2,1)S(1)}, bf16[4,128,128]{2,1,0:T(8,128)(2,1)S(1)}, u32[]{:S(2)}, u32[]{:S(2)}) collective-permute-start(bf16[4,128,128]{2,1,0:T(8,128)(2,1)S(1)} %bitcast.278), channel_id=1, source_target_pairs={{0,16},{4,20},{8,24},{12,28},{16,0},{20,4},{24,8},{28,12},{1,17},{... | collective-permute-start | bytes 393224 | tf_op jit(solution)/shard_map/ppermute | solution.py:18
  27.9 9.4 %collective-permute-start.11 = (bf16[4,128,128]{2,1,0:T(8,128)(2,1)S(1)}, bf16[4,128,128]{2,1,0:T(8,128)(2,1)S(1)}, u32[]{:S(2)}, u32[]{:S(2)}) collective-permute-start(bf16[4,128,128]{2,1,0:T(8,128)(2,1)S(1)} %bitcast.282), channel_id=1, source_target_pairs={{0,16},{4,20},{8,24},{12,28},{16,0},{20,4},{24,8},{28,12},{1,17},{... | collective-permute-start | bytes 393224 | tf_op jit(solution)/shard_map/ppermute | solution.py:18
  38.3 39.6 %copy-start.2 = (bf16[6,128,128]{2,1,0:T(8,128)(2,1)S(1)}, bf16[6,128,128]{2,1,0:T(8,128)(2,1)}, u32[]{:S(2)}) copy-start(bf16[6,128,128]{2,1,0:T(8,128)(2,1)} %param.10) | copy-start | bytes 589828
  38.3 101.8 %all-reduce.5.cloned.1.call-start = ((), (), s32[]{:S(2)}) async-start(), calls=%async_computation | async-start | bytes 1310720 | tf_op jit(solution)/shard_map/psum | solution.py:119
  76.1 1.8 %copy-start.1 = (f32[128,128]{0,1:T(8,128)S(1)}, f32[128,128]{0,1:T(8,128)}, u32[]{:S(2)}) copy-start(f32[128,128]{0,1:T(8,128)} %get-tuple-element.10) | copy-start | bytes 196612
  76.1 1.8 %copy-start.9 = (f32[128,128]{0,1:T(8,128)S(1)}, f32[128,128]{0,1:T(8,128)}, u32[]{:S(2)}) copy-start(f32[128,128]{0,1:T(8,128)} %get-tuple-element.11) | copy-start | bytes 196612
  77.9 0.8 copy-start.8
  80.6 0.8 copy-start.7
  84.6 55.5 %copy-start.4 = (f32[4,128,128]{2,1,0:T(8,128)S(1)}, f32[4,128,128]{2,1,0:T(8,128)}, u32[]{:S(2)}) copy-start(f32[4,128,128]{2,1,0:T(8,128)} %param.11) | copy-start | bytes 786436
  140.1 1.0 copy-start.6
  141.1 0.9 copy-start.5
  142.6 1.0 copy-start.3
Sparse Core Ops, SparseCore 0:
  38.4 37.6 all-reduce.6
  84.7 55.3 all-reduce.4
